TPU v7x, 32 devices: a whole 2x2x4 slice. The times are simulated.
32 devices in a mesh: user: 8 (over y, x, core), item: 4 (over z).
Axes of the slice: x: 2, y: 2, z: 4, core: 2. Of those that a mesh axis runs over, the one named last changes fastest.
Arguments:
- user_factors: float32 [4096, 256], P('user'), may hold values from -1.5 to 1.5
- item_factors: float32 [32768, 256], P(('user', 'item')), may hold values from -1.5 to 1.5
- feedback: bfloat16 [128, 4096, 128], P('item', 'user'), may hold values from 0 to 1
- item_pick: int32 [32, 32], replicated, may hold values from 0 to 7, as said below
- user_noise: float32 [4096, 256], P('user'), may hold values from -6 to 6
- item_noise: float32 [32768, 256], P(('user', 'item')), may hold values from -6 to 6
Outputs:
- new_user: float32 [4096, 256], P('user')
- new_item: float32 [32768, 256], P(('user', 'item'))
Inputs may be any that keep to these rules, and one draw needn't show every extreme that they name: For every owner o and every user slab u, the 4 entries item_pick[u * 4 + i, o] are distinct, so that no tile appears twice.
All inputs are finite; a program needn't handle non-finite values.
Results may differ from a plain program's by a relative error of at most 0.00058.
Values may be sent and summed in bfloat16 or wider, within the bound.
A program may use at most 192 MiB of HBM per device.

v0:
```python
import math

import jax
import jax.numpy as jnp
from jax import lax
from jax.sharding import PartitionSpec as P

step_size = 0.01
item_step = 0.1
prior_weight = 1.0
noise_scale = math.sqrt(0.02)
item_noise_scale = math.sqrt(0.2)


def local(user_factors, item_factors, feedback, item_pick, user_noise, item_noise):
    devices = lax.axis_size(("user", "item"))
    own_index = lax.axis_index(("user", "item"))
    tile_size = feedback.shape[2]
    rank_width = item_factors.shape[1]
    held_blocks = item_factors.shape[0] // tile_size
    item_half = item_factors.astype(jnp.bfloat16).reshape(held_blocks, tile_size, rank_width)
    wanted = lax.dynamic_slice_in_dim(item_pick, own_index, 1, 1)[:, 0]
    outgoing = jnp.take(item_half, wanted, axis=0)
    arrived = lax.all_to_all(outgoing, ("user", "item"), split_axis=0, concat_axis=0, tiled=True)
    user_slab = user_factors.astype(jnp.bfloat16)
    scores = jnp.einsum("uk,ntk->nut", user_slab, arrived, preferred_element_type=jnp.float32)
    residual = (jax.nn.sigmoid(scores) - feedback.astype(jnp.float32)).astype(jnp.bfloat16)
    user_grad = jnp.einsum("nut,ntk->uk", residual, arrived, preferred_element_type=jnp.float32)
    item_part = jnp.einsum("nut,uk->ntk", residual, user_slab, preferred_element_type=jnp.float32)
    returned = lax.all_to_all(
        item_part, ("user", "item"), split_axis=0, concat_axis=0, tiled=True
    ).reshape(devices, tile_size * rank_width)
    selector = (wanted[None, :] == jnp.arange(held_blocks, dtype=jnp.int32)[:, None]).astype(
        jnp.float32
    )
    item_grad = jnp.dot(
        selector, returned, precision=lax.Precision.HIGHEST, preferred_element_type=jnp.float32
    ).reshape(item_factors.shape)
    new_item = (
        item_factors
        - item_step * (item_grad + prior_weight * item_factors)
        + item_noise_scale * item_noise
    )
    grad_total = lax.psum(user_grad, "item")
    new_user = (
        user_factors
        - step_size * (grad_total + prior_weight * user_factors)
        + noise_scale * user_noise
    )
    return (new_user, new_item)


def solution(mesh):
    in_specs = (
        P("user", None),
        P(("user", "item"), None),
        P("item", "user", None),
        P(),
        P("user", None),
        P(("user", "item"), None),
    )
    out_specs = (P("user", None), P(("user", "item"), None))
    return jax.shard_map(local, mesh=mesh, in_specs=in_specs, out_specs=out_specs, check_vma=False)
```

profile of v0, /device:TPU:0, one launch (start us, length us, event | category | flops | bytes accessed | tf_op | source)
XLA Modules:
  0.0 203.6 jit_solution(1863423456064665915)
XLA Ops:
  7.2 0.9 and_reduce_fusion
  8.1 0.9 dynamic-slice_reduce_fusion
  9.0 1.3 convert_element_type.13
  10.3 0.7 gather_fusion
  11.0 1.6 broadcast_select_fusion
  12.5 7.3 %all-to-all-start = ((bf16[32,128,256]{2,1,0:T(8,128)(2,1)}), bf16[32,128,256]{2,1,0:T(8,128)(2,1)S(1)}, u32[]{:S(2)}, u32[]{:S(2)}) async-start(bf16[32,128,256]{2,1,0:T(8,128)(2,1)} %broadcast_select_fusion), calls=%async_computation | async-start | bytes 4194304 | tf_op jit(solution)/shard_map/all_to_all | solution.py:24
  19.9 0.0 copy-start.2
  19.9 6.5 %copy.10 = bf16[32,512,128]{1,2,0:T(8,128)(2,1)} copy(bf16[32,512,128]{2,1,0:T(8,128)(2,1)} %param.8) | data formatting | bytes 8388608 | tf_op args[2]
  26.4 40.4 %all-to-all-done = bf16[32,128,256]{2,1,0:T(8,128)(2,1)S(1)} async-done(((bf16[32,128,256]{2,1,0:T(8,128)(2,1)}), bf16[32,128,256]{2,1,0:T(8,128)(2,1)S(1)}, u32[]{:S(2)}, u32[]{:S(2)}) %all-to-all-start) | async-done | bytes 2097184 | tf_op jit(solution)/shard_map/all_to_all | solution.py:24
  66.8 0.0 copy-done.2
  66.8 4.2 %fusion = bf16[32,512,128]{1,2,0:T(8,128)(2,1)S(1)} fusion(bf16[32,512,128]{1,2,0:T(8,128)(2,1)} %copy.10, bf16[32,128,256]{2,1,0:T(8,128)(2,1)S(1)} %all-to-all-done, f32[512,256]{1,0:T(8,128)S(1)} %copy-done.2), kind=kOutput, calls=%fused_computation.2 | convolution fusion | flops 1086455808 | bytes 11010048 | tf_op jit(solution)/shard_map/uk,ntk->nut/dot_general | solution.py:26
  71.0 0.0 copy-start
  71.0 2.0 copy-done
  73.0 3.2 %fusion.1 = f32[32,128,256]{2,1,0:T(8,128)} fusion(bf16[32,512,128]{1,2,0:T(8,128)(2,1)S(1)} %fusion, f32[512,256]{1,0:T(8,128)S(1)} %copy-done.2), kind=kOutput, calls=%fused_computation.7 | convolution fusion | flops 1073872896 | bytes 8912896 | tf_op jit(solution)/shard_map/nut,uk->ntk/dot_general | solution.py:29
  76.2 4.7 %all-to-all-start.1 = ((f32[32,128,256]{2,1,0:T(8,128)}), f32[32,128,256]{2,1,0:T(8,128)}, u32[]{:S(2)}, u32[]{:S(2)}) async-start(f32[32,128,256]{2,1,0:T(8,128)} %fusion.1), calls=%async_computation.1 | async-start | bytes 8388608 | tf_op jit(solution)/shard_map/all_to_all | solution.py:30
  80.9 0.0 copy-start.3
  80.9 0.0 all-reduce.2.cloned.1.call-start
  81.0 4.3 %convolution_bitcast_fusion = f32[512,256]{1,0:T(8,128)} fusion(bf16[32,512,128]{1,2,0:T(8,128)(2,1)} %copy-done, bf16[32,128,256]{2,1,0:T(8,128)(2,1)S(1)} %all-to-all-done), kind=kOutput, calls=%fused_computation.4 | convolution fusion | flops 1073741824 | bytes 6815744 | tf_op jit(solution)/shard_map/nut,ntk->uk/dot_general | solution.py:28
  85.3 0.0 all-reduce.2.cloned.1.call-update
  85.3 58.2 %all-reduce.2.cloned.1.call-done = f32[512,256]{1,0:T(8,128)} async-done(((f32[512,256]{1,0:T(8,128)}), f32[512,256]{1,0:T(8,128)}) %all-reduce.2.cloned.1.call-update) | async-done | bytes 524304 | tf_op jit(solution)/shard_map/psum | solution.py:44
  143.6 0.0 copy-done.3
  143.6 1.9 multiply_add_fusion.1
  145.5 42.5 %all-to-all-done.1 = f32[32,128,256]{2,1,0:T(8,128)} async-done(((f32[32,128,256]{2,1,0:T(8,128)}), f32[32,128,256]{2,1,0:T(8,128)}, u32[]{:S(2)}, u32[]{:S(2)}) %all-to-all-start.1) | async-done | bytes 4194336 | tf_op jit(solution)/shard_map/all_to_all | solution.py:30
  188.0 4.6 %copy.13 = f32[4,8,128,256]{3,1,2,0:T(8,128)S(1)} copy(f32[4,8,128,256]{3,2,1,0:T(8,128)} %bitcast.4) | data formatting | bytes 8388608
  192.7 0.0 copy-start.1
  192.7 1.5 fusion.7
  194.2 0.2 reshape.20
  194.4 0.0 copy-done.1
  194.4 2.4 %multiply_add_fusion = f32[1024,256]{1,0:T(8,128)} fusion(f32[1024,256]{1,0:T(8,128)} %param.11, f32[1024,256]{1,0:T(8,128)S(1)} %copy-done.1, f32[1024,256]{1,0:T(8,128)S(1)} %reshape.20), kind=kLoop, calls=%fused_computation.5 | loop fusion | flops 1310720 | bytes 4194304 | tf_op jit(solution)/shard_map/add | solution.py:40
  (1 shorter events, 0.0 us)
Async XLA Ops:
  12.5 54.2 %all-to-all-start = ((bf16[32,128,256]{2,1,0:T(8,128)(2,1)}), bf16[32,128,256]{2,1,0:T(8,128)(2,1)S(1)}, u32[]{:S(2)}, u32[]{:S(2)}) async-start(bf16[32,128,256]{2,1,0:T(8,128)(2,1)} %broadcast_select_fusion), calls=%async_computation | async-start | bytes 4194304 | tf_op jit(solution)/shard_map/all_to_all | solution.py:24
  19.9 46.9 %copy-start.2 = (f32[512,256]{1,0:T(8,128)S(1)}, f32[512,256]{1,0:T(8,128)}, u32[]{:S(2)}) copy-start(f32[512,256]{1,0:T(8,128)} %param.6) | copy-start | bytes 1572868
  71.0 2.0 copy-start
  76.2 111.8 %all-to-all-start.1 = ((f32[32,128,256]{2,1,0:T(8,128)}), f32[32,128,256]{2,1,0:T(8,128)}, u32[]{:S(2)}, u32[]{:S(2)}) async-start(f32[32,128,256]{2,1,0:T(8,128)} %fusion.1), calls=%async_computation.1 | async-start | bytes 8388608 | tf_op jit(solution)/shard_map/all_to_all | solution.py:30
  80.9 62.6 %copy-start.3 = (f32[512,256]{1,0:T(8,128)S(1)}, f32[512,256]{1,0:T(8,128)}, u32[]{:S(2)}) copy-start(f32[512,256]{1,0:T(8,128)} %param.10) | copy-start | bytes 1572868
  80.9 62.6 %all-reduce.2.cloned.1.call-start = ((), (), s32[]{:S(2)}) async-start(), calls=%async_computation.2 | async-start | bytes 1048576 | tf_op jit(solution)/shard_map/psum | solution.py:44
  192.7 1.7 copy-start.1
Sparse Core Ops, SparseCore 0:
  85.5 58.0 all-reduce.1
where the time goes:
time: 206 us; the launch traced here: 204 us
  waiting for transfers between devices  141 us (68%)
  between operations  14.1 us (7%)
  local copies, waits for them, and re-layouts  14 us (7%)
  matrix products  13.3 us (6%)
  starting transfers between devices  12.1 us (6%)
  other arithmetic  9.02 us (4%)
    psum x1, waiting for transfers between devices, local(): grad_total = lax.psum(user_grad, 'item')  58.2 us
    all_to_all x1, waiting for transfers between devices, local(): lax.all_to_all(item_part, ('user', 'item'), split_axis=0, concat_axis=0,...  42.5 us
    all_to_all x1, waiting for transfers between devices, local(): lax.all_to_all(outgoing, ('user', 'item'), split_axis=0, concat_axis=0, t...  40.4 us
    unnamed x10, local copies, waits for them, and re-layouts  13.1 us
    all_to_all x1, starting transfers between devices, local(): lax.all_to_all(outgoing, ('user', 'item'), split_axis=0, concat_axis=0, t...  7.33 us
    all_to_all x1, starting transfers between devices, local(): lax.all_to_all(item_part, ('user', 'item'), split_axis=0, concat_axis=0,...  4.7 us
    dot_general x1, matrix products, local(): jnp.einsum('nut,ntk->uk', residual, arrived, preferred_element_type=jnp.f...  4.31 us
    dot_general x1, matrix products, local(): jnp.einsum('uk,ntk->nut', user_slab, arrived, preferred_element_type=jnp....  4.23 us
  transfers between devices with their start and end apart: 3, of which 3 were waited for; matrix products, arithmetic and copies ran while one was open for 6% of the time, Pallas kernels for 0%

commit v1 on v0

--- a/solution.py
+++ b/solution.py
@@ -28,8 +28,8 @@
     user_grad = jnp.einsum("nut,ntk->uk", residual, arrived, preferred_element_type=jnp.float32)
     item_part = jnp.einsum("nut,uk->ntk", residual, user_slab, preferred_element_type=jnp.float32)
     returned = lax.all_to_all(
-        item_part, ("user", "item"), split_axis=0, concat_axis=0, tiled=True
-    ).reshape(devices, tile_size * rank_width)
+        item_part.astype(jnp.float16), ("user", "item"), split_axis=0, concat_axis=0, tiled=True
+    ).astype(jnp.float32).reshape(devices, tile_size * rank_width)
     selector = (wanted[None, :] == jnp.arange(held_blocks, dtype=jnp.int32)[:, None]).astype(
         jnp.float32
     )

time: 206 us -> 158 us (0.77)
  waiting for transfers between devices: 141 us -> 97.1 us
  local copies, waits for them, and re-layouts: 14 us -> 10.9 us
    all_to_all x1, waiting for transfers between devices: 42.5 us -> 1.83 us  [local(): lax.all_to_all(item_part.astype(jnp.float16), ('user', 'item'), split_axi...]
    psum x1, waiting for transfers between devices: 58.2 us -> 54.9 us  [local(): grad_total = lax.psum(user_grad, 'item')]
    unnamed x10 -> x12, local copies, waits for them, and re-layouts: 13.1 us -> 10 us
  transfers between devices with their start and end apart: 3 -> 3, of which waited for: 3 -> 3; matrix products, arithmetic and copies ran while one was open for 6% -> 9% of each run, Pallas kernels for 0% -> 0%
where the time goes in v1:
time: 158 us; the launch traced here: 156 us
  waiting for transfers between devices  97.1 us (61%)
  between operations  14.1 us (9%)
  matrix products  13.4 us (8%)
  starting transfers between devices  11.9 us (8%)
  local copies, waits for them, and re-layouts  10.9 us (7%)
  other arithmetic  9.02 us (6%)
    psum x1, waiting for transfers between devices, local(): grad_total = lax.psum(user_grad, 'item')  54.9 us
    all_to_all x1, waiting for transfers between devices, local(): lax.all_to_all(outgoing, ('user', 'item'), split_axis=0, concat_axis=0, t...  40.4 us
    unnamed x12, local copies, waits for them, and re-layouts  10 us
    all_to_all x1, starting transfers between devices, local(): lax.all_to_all(outgoing, ('user', 'item'), split_axis=0, concat_axis=0, t...  7.33 us
    dot_general x1, matrix products, local(): jnp.einsum('nut,ntk->uk', residual, arrived, preferred_element_type=jnp.f...  4.98 us
    dot_general x1, matrix products, local(): jnp.einsum('uk,ntk->nut', user_slab, arrived, preferred_element_type=jnp....  4.98 us
    all_to_all x1, starting transfers between devices, local(): lax.all_to_all(item_part.astype(jnp.float16), ('user', 'item'), split_axi...  4.58 us
  transfers between devices with their start and end apart: 3, of which 3 were waited for; matrix products, arithmetic and copies ran while one was open for 9% of the time, Pallas kernels for 0%

profile of v1, /device:TPU:0, one launch (start us, length us, event | category | flops | bytes accessed | tf_op | source)
XLA Modules:
  0.0 156.5 jit_solution(5544811581886547862)
XLA Ops:
  7.2 0.9 and_reduce_fusion
  8.1 0.9 dynamic-slice_reduce_fusion
  9.0 1.3 convert_element_type.17
  10.3 0.7 gather_fusion
  11.0 1.6 %broadcast_select_fusion = bf16[32,128,256]{2,1,0:T(8,128)(2,1)} fusion(bf16[32,128,256]{2,1,0:T(8,128)(2,1)S(1)} %gather_fusion, pred[32]{0:T(512)(128)(4,1)S(1)} %and_reduce_fusion), kind=kLoop, calls=%fused_computation.3 | loop fusion | flops 1048576 | bytes 4194336 | tf_op jit(solution)/shard_map/jit(_take)/select_n | solution.py:23
  12.5 7.3 %all-to-all-start = ((bf16[32,128,256]{2,1,0:T(8,128)(2,1)}), bf16[32,128,256]{2,1,0:T(8,128)(2,1)S(1)}, u32[]{:S(2)}, u32[]{:S(2)}) async-start(bf16[32,128,256]{2,1,0:T(8,128)(2,1)} %broadcast_select_fusion), calls=%async_computation | async-start | bytes 4194304 | tf_op jit(solution)/shard_map/all_to_all | solution.py:24
  19.9 0.0 copy-start.3
  19.9 6.5 %copy.10 = bf16[32,512,128]{1,2,0:T(8,128)(2,1)} copy(bf16[32,512,128]{2,1,0:T(8,128)(2,1)} %param.8) | data formatting | bytes 8388608 | tf_op args[2]
  26.4 40.4 %all-to-all-done = bf16[32,128,256]{2,1,0:T(8,128)(2,1)S(1)} async-done(((bf16[32,128,256]{2,1,0:T(8,128)(2,1)}), bf16[32,128,256]{2,1,0:T(8,128)(2,1)S(1)}, u32[]{:S(2)}, u32[]{:S(2)}) %all-to-all-start) | async-done | bytes 2097184 | tf_op jit(solution)/shard_map/all_to_all | solution.py:24
  66.8 0.0 copy-done.3
  66.8 0.0 copy-start.2
  66.8 5.0 %fusion = bf16[32,512,128]{1,2,0:T(8,128)(2,1)S(1)} fusion(bf16[32,512,128]{1,2,0:T(8,128)(2,1)} %copy.10, bf16[32,128,256]{2,1,0:T(8,128)(2,1)S(1)} %all-to-all-done, f32[512,256]{1,0:T(8,128)S(1)} %copy-done.3), kind=kOutput, calls=%fused_computation.2 | convolution fusion | flops 1086455808 | bytes 11010048 | tf_op jit(solution)/shard_map/uk,ntk->nut/dot_general | solution.py:26
  71.8 0.0 copy-done.2
  71.8 0.0 copy-start
  71.8 1.9 %copy-done = bf16[32,512,128]{1,2,0:T(8,128)(2,1)} copy-done((bf16[32,512,128]{1,2,0:T(8,128)(2,1)}, bf16[32,512,128]{1,2,0:T(8,128)(2,1)S(1)}, u32[]{:S(2)}) %copy-start) | copy-done | bytes 4194328
  73.7 2.6 %convolution_convert_fusion = f16[32,128,256]{2,1,0:T(8,128)(2,1)} fusion(bf16[32,512,128]{1,2,0:T(8,128)(2,1)S(1)} %fusion, f32[512,256]{1,0:T(8,128)S(1)} %copy-done.3), kind=kOutput, calls=%fused_computation.4 | convolution fusion | flops 1074921472 | bytes 6815744 | tf_op jit(solution)/shard_map/nut,uk->ntk/dot_general | solution.py:29
  76.3 4.6 %all-to-all-start.1 = ((f16[32,128,256]{2,1,0:T(8,128)(2,1)}), f16[32,128,256]{2,1,0:T(8,128)(2,1)S(1)}, u32[]{:S(2)}, u32[]{:S(2)}) async-start(f16[32,128,256]{2,1,0:T(8,128)(2,1)} %convolution_convert_fusion), calls=%async_computation.1 | async-start | bytes 4194304 | tf_op jit(solution)/shard_map/all_to_all | solution.py:30
  80.9 0.0 copy-start.4
  80.9 0.0 all-reduce.2.cloned.1.call-start
  80.9 5.0 %convolution_bitcast_fusion = f32[512,256]{1,0:T(8,128)} fusion(bf16[32,512,128]{1,2,0:T(8,128)(2,1)} %copy-done, bf16[32,128,256]{2,1,0:T(8,128)(2,1)} %copy-done.2), kind=kOutput, calls=%fused_computation.5 | convolution fusion | flops 1073741824 | bytes 6815744 | tf_op jit(solution)/shard_map/nut,ntk->uk/dot_general | solution.py:28
  85.9 0.0 all-reduce.2.cloned.1.call-update
  86.0 54.9 %all-reduce.2.cloned.1.call-done = f32[512,256]{1,0:T(8,128)} async-done(((f32[512,256]{1,0:T(8,128)}), f32[512,256]{1,0:T(8,128)}) %all-reduce.2.cloned.1.call-update) | async-done | bytes 524304 | tf_op jit(solution)/shard_map/psum | solution.py:44
  140.8 0.0 copy-done.4
  140.8 1.9 %multiply_add_fusion.1 = f32[512,256]{1,0:T(8,128)} fusion(f32[512,256]{1,0:T(8,128)S(1)} %copy-done.4, f32[512,256]{1,0:T(8,128)S(1)} %copy-done.3, f32[512,256]{1,0:T(8,128)} %all-reduce.2.cloned.1.call-done), kind=kLoop, calls=%fused_computation.7 | loop fusion | flops 655360 | bytes 2097152 | tf_op jit(solution)/shard_map/add | solution.py:46
  142.8 1.8 %all-to-all-done.1 = f16[32,128,256]{2,1,0:T(8,128)(2,1)S(1)} async-done(((f16[32,128,256]{2,1,0:T(8,128)(2,1)}), f16[32,128,256]{2,1,0:T(8,128)(2,1)S(1)}, u32[]{:S(2)}, u32[]{:S(2)}) %all-to-all-start.1) | async-done | bytes 2097184 | tf_op jit(solution)/shard_map/all_to_all | solution.py:30
  144.6 1.4 copy.13
  146.0 0.0 copy-start.1
  146.0 0.9 fusion.6
  146.9 0.2 reshape.20
  147.0 0.2 copy-done.1
  147.2 2.4 %multiply_add_fusion = f32[1024,256]{1,0:T(8,128)} fusion(f32[1024,256]{1,0:T(8,128)} %param.11, f32[1024,256]{1,0:T(8,128)S(1)} %copy-done.1, f32[1024,256]{1,0:T(8,128)S(1)} %reshape.20), kind=kLoop, calls=%fused_computation.6 | loop fusion | flops 1310720 | bytes 4194304 | tf_op jit(solution)/shard_map/add | solution.py:40
  (1 shorter events, 0.0 us)
Async XLA Ops:
  12.5 54.2 %all-to-all-start = ((bf16[32,128,256]{2,1,0:T(8,128)(2,1)}), bf16[32,128,256]{2,1,0:T(8,128)(2,1)S(1)}, u32[]{:S(2)}, u32[]{:S(2)}) async-start(bf16[32,128,256]{2,1,0:T(8,128)(2,1)} %broadcast_select_fusion), calls=%async_computation | async-start | bytes 4194304 | tf_op jit(solution)/shard_map/all_to_all | solution.py:24
  19.9 46.9 %copy-start.3 = (f32[512,256]{1,0:T(8,128)S(1)}, f32[512,256]{1,0:T(8,128)}, u32[]{:S(2)}) copy-start(f32[512,256]{1,0:T(8,128)} %param.6) | copy-start | bytes 1572868
  66.8 5.0 %copy-start.2 = (bf16[32,128,256]{2,1,0:T(8,128)(2,1)}, bf16[32,128,256]{2,1,0:T(8,128)(2,1)S(1)}, u32[]{:S(2)}) copy-start(bf16[32,128,256]{2,1,0:T(8,128)(2,1)S(1)} %all-to-all-done) | copy-start | bytes 6291460
  71.8 1.9 %copy-start = (bf16[32,512,128]{1,2,0:T(8,128)(2,1)}, bf16[32,512,128]{1,2,0:T(8,128)(2,1)S(1)}, u32[]{:S(2)}) copy-start(bf16[32,512,128]{1,2,0:T(8,128)(2,1)S(1)} %fusion) | copy-start | bytes 12582916
  76.3 68.3 %all-to-all-start.1 = ((f16[32,128,256]{2,1,0:T(8,128)(2,1)}), f16[32,128,256]{2,1,0:T(8,128)(2,1)S(1)}, u32[]{:S(2)}, u32[]{:S(2)}) async-start(f16[32,128,256]{2,1,0:T(8,128)(2,1)} %convolution_convert_fusion), calls=%async_computation.1 | async-start | bytes 4194304 | tf_op jit(solution)/shard_map/all_to_all | solution.py:30
  80.9 60.0 %copy-start.4 = (f32[512,256]{1,0:T(8,128)S(1)}, f32[512,256]{1,0:T(8,128)}, u32[]{:S(2)}) copy-start(f32[512,256]{1,0:T(8,128)} %param.10) | copy-start | bytes 1572868
  80.9 60.0 %all-reduce.2.cloned.1.call-start = ((), (), s32[]{:S(2)}) async-start(), calls=%async_computation.2 | async-start | bytes 1048576 | tf_op jit(solution)/shard_map/psum | solution.py:44
  146.0 1.2 copy-start.1
Sparse Core Ops, SparseCore 0:
  86.1 54.7 all-reduce.1

commit v2 on v1

v2 whole, which is shorter than its diff:
```python
import functools
import math

import jax
import jax.numpy as jnp
from jax import lax
from jax.experimental import pallas as pl
from jax.experimental.pallas import tpu as pltpu
from jax.sharding import PartitionSpec as P

step_size = 0.01
item_step = 0.1
prior_weight = 1.0
noise_scale = math.sqrt(0.02)
item_noise_scale = math.sqrt(0.2)

FACTOR_BOUND = 1.5
LEVELS = 32766.0
PAD = 16


def encode(ref, value, unit):
    rows = value.shape[0]
    largest = jnp.max(jnp.abs(value), axis=0, keepdims=True)
    count = jnp.floor(largest * (1.0 / (LEVELS * unit))) + 1.0
    inverse = 1.0 / (count * unit)
    ref[pl.ds(0, rows), :] = jnp.round(value * inverse).astype(jnp.int32).astype(jnp.int16)
    ref[pl.ds(rows, PAD), :] = jnp.broadcast_to(count, (PAD, value.shape[1])).astype(jnp.int32).astype(jnp.int16)


def decode(ref, weight):
    rows = ref.shape[0] - PAD
    count = ref[pl.ds(rows, PAD), :].astype(jnp.float32)[0:1]
    return ref[pl.ds(0, rows), :].astype(jnp.float32) * (count * weight)


def kernel(
    U, Z, pick, items, user, feedback, item_out, user_out, *scratch
):
    zbufs = scratch[: 2 * (Z - 1)]
    (og, arr, gs, gr, cs, cr, crd, fb, us, ur, ugs, ugr, ug, zsend, zrecv, isend, irecv, gsend, grecv,
     csend, crecv, cdrecv, fsem, usend, urecv, vsend, vrecv) = scratch[2 * (Z - 1):]
    B, T, K = items.shape
    N = user.shape[0]
    piece = N // Z
    me = lax.axis_index("user")
    z = lax.axis_index("item")
    item_unit = N * FACTOR_BOUND * U / LEVELS / 32000.0
    user_unit = U * Z * T * FACTOR_BOUND * Z / LEVELS / 32000.0

    def far(axis, to, src, dst, ssem, rsem):
        return pltpu.make_async_remote_copy(
            src_ref=src, dst_ref=dst, send_sem=ssem, recv_sem=rsem,
            device_id={axis: to}, device_id_type=pl.DeviceIdType.MESH)

    barrier = pltpu.get_barrier_semaphore()

    def greet_user(j, c):
        pl.semaphore_signal(barrier, inc=1, device_id={"user": lax.rem(me + j, U)}, device_id_type=pl.DeviceIdType.MESH)
        return c

    lax.fori_loop(1, U, greet_user, 0)
    for j in range(1, Z):
        pl.semaphore_signal(barrier, inc=1, device_id={"item": lax.rem(z + j, Z)}, device_id_type=pl.DeviceIdType.MESH)
    pl.semaphore_wait(barrier, U - 1 + Z - 1)

    def zcopy(d, way):
        src = items if d == 1 else zbufs[2 * (d - 2) + way]
        k = 2 * (d - 1) + way
        return far("item", z + (1 if way == 0 else -1), src, zbufs[k], zsend.at[k], zrecv.at[k])

    def can_send(d, way):
        return (z - (d - 1) >= 0) & (z + 1 < Z) if way == 0 else (z + (d - 1) < Z) & (z >= 1)

    def comes(d, way):
        return z - d >= 0 if way == 0 else z + d < Z

    for way in (0, 1):
        pl.when(can_send(1, way))(lambda way=way: zcopy(1, way).start())

    ug[...] = jnp.zeros_like(ug)

    def icopy(p, to, src):
        return far("user", to, og.at[p, to], arr.at[p, src], isend.at[p, to], irecv.at[p, src])

    def spread(p, blocks):
        def one(j, c):
            to = lax.rem(me + j, U)
            og[p, to] = blocks[pick[to * Z + z, me * Z + p]]
            icopy(p, to, me).start()
            return c
        lax.fori_loop(1, U, one, 0)
        arr[p, me] = blocks[pick[me * Z + z, me * Z + p]]

    def gcopy(p, to, src):
        return far("user", to, gs.at[p, to], gr.at[p, src], gsend.at[p, to], grecv.at[p, src])

    def fcopy(p, pair, slot):
        return pltpu.make_async_copy(feedback.at[pl.ds(2 * pair, 2), p], fb.at[slot], fsem.at[slot])

    pairs = U // 2

    def pair_of(j):
        return lax.rem(me // 2 + 1 + j, pairs)

    def compute(p):
        fcopy(p, pair_of(0), 0).start()

        def one(j, c):
            pair = pair_of(j)
            slot = lax.rem(j, 2)

            @pl.when(j + 1 < pairs)
            def _():
                fcopy(p, pair_of(j + 1), 1 - slot).start()

            for t in range(2):
                o = 2 * pair + t
                pl.when(o != me)(lambda o=o: icopy(p, me, o).wait_recv())
            fcopy(p, pair, slot).wait()
            tile = arr[p, pl.ds(2 * pair, 2)].reshape(2 * T, K)
            scores = lax.dot_general(user[...], tile, (((1,), (1,)), ((), ())), preferred_element_type=jnp.float32)
            target = jnp.concatenate([fb[slot, 0], fb[slot, 1]], axis=1).astype(jnp.float32)
            residual = (0.5 * jnp.tanh(0.5 * scores) + (0.5 - target)).astype(jnp.bfloat16)
            part = lax.dot_general(residual, user[...], (((0,), (0,)), ((), ())), preferred_element_type=jnp.float32)
            for t in range(2):
                o = 2 * pair + t
                value = part[t * T:(t + 1) * T]

                @pl.when(o != me)
                def _():
                    encode(gs.at[p, o], value, item_unit)
                    gcopy(p, o, me).start()

                @pl.when(o == me)
                def _():
                    encode(gr.at[p, me], value, item_unit)
            ug[...] += jnp.dot(residual, tile, preferred_element_type=jnp.float32)
            return c

        lax.fori_loop(0, pairs, one, 0)

    def dense(p, b):
        def one(u, acc):
            weight = jnp.where(pick[u * Z + z, me * Z + p] == b, item_unit, 0.0).astype(jnp.float32)
            return acc + decode(gr.at[p, u], weight)
        return lax.fori_loop(0, U, one, jnp.zeros((T, K), jnp.float32))

    def await_grads(p):
        def one(j, c):
            gcopy(p, me, lax.rem(me + j, U)).wait_recv()
            return c
        lax.fori_loop(1, U, one, 0)

    def chain(p, way, relay):
        await_grads(p)
        to = z + (1 if way == 0 else -1)

        def one(b, c):
            total = dense(p, b)
            if relay:
                far("item", z, cs.at[p, b], cr.at[p, b], csend.at[p, b], crecv.at[p, b]).wait_recv()
                total = total + decode(cr.at[p, b], item_unit)
            encode(cs.at[p, b], total, item_unit)
            if way == 0:
                far("item", to, cs.at[p, b], cr.at[p, b], csend.at[p, b], crecv.at[p, b]).start()
            else:
                @pl.when(to == p)
                def _():
                    far("item", to, cs.at[p, b], crd.at[b], csend.at[p, b], cdrecv.at[b]).start()

                @pl.when(to != p)
                def _():
                    far("item", to, cs.at[p, b], cr.at[p, b], csend.at[p, b], crecv.at[p, b]).start()
            return c
        lax.fori_loop(0, B, one, 0)

    def plane(d, way):
        return z - d if way == 0 else z + d

    def start_chain(d, way):
        out = 1 - way
        edge = z == 0 if out == 0 else z == Z - 1

        @pl.when(comes(d, way) & edge)
        def _():
            chain(plane(d, way), out, False)

    steps = [(d, way) for d in range(1, Z) for way in (0, 1)]
    spread(z, items)
    last = None
    older = None
    compute_own = True
    for d in range(1, Z):
        for way in (0, 1):
            @pl.when(comes(d, way))
            def _(d=d, way=way):
                zcopy(d, way).wait_recv()
                if d + 1 < Z:
                    pl.when(can_send(d + 1, way))(lambda: zcopy(d + 1, way).start())
                spread(plane(d, way), zbufs[2 * (d - 1) + way])
        if d == 1:
            compute(z)
        else:
            for way in (0, 1):
                pl.when(comes(d - 1, way))(lambda d=d, way=way: compute(plane(d - 1, way)))
        if d > 2:
            for way in (0, 1):
                start_chain(d - 2, way)
    for way in (0, 1):
        pl.when(comes(Z - 1, way))(lambda way=way: compute(plane(Z - 1, way)))

    def ucopy(to, src):
        return far("item", to, us.at[to], ur.at[src], usend.at[to], urecv.at[src])

    for j in range(1, Z):
        to = lax.rem(z + j, Z)
        encode(us.at[to], ug[pl.ds(pl.multiple_of(to * piece, piece), piece), :], user_unit)
        ucopy(to, z).start()
    for d in range(max(Z - 2, 1), Z):
        for way in (0, 1):
            start_chain(d, way)

    def vcopy(to, src, j):
        return far("item", to, ugs, ugr.at[src], vsend.at[j], vrecv.at[src])

    total = ug[pl.ds(pl.multiple_of(z * piece, piece), piece), :]
    for j in range(1, Z):
        src = lax.rem(z + j, Z)
        ucopy(z, src).wait_recv()
        total = total + decode(ur.at[src], user_unit)
    encode(ugs, total, user_unit)
    for j in range(1, Z):
        vcopy(lax.rem(z + j, Z), z, j - 1).start()
    user_out[pl.ds(pl.multiple_of(z * piece, piece), piece), :] = decode(ugs, user_unit)

    for d in range(1, Z):
        pl.when((z > 0) & (z + d < Z))(lambda d=d: chain(z + d, 0, True))
    for d in range(1, Z):
        pl.when((z < Z - 1) & (z - d >= 0))(lambda d=d: chain(z - d, 1, True))

    await_grads(z)

    def finish(b, c):
        item_out[b] = dense(z, b)

        @pl.when(z > 0)
        def _():
            far("item", z, cs.at[z, b], cr.at[z, b], csend.at[z, b], crecv.at[z, b]).wait_recv()
            item_out[b] += decode(cr.at[z, b], item_unit)

        @pl.when(z < Z - 1)
        def _():
            far("item", z, cs.at[z, b], crd.at[b], csend.at[z, b], cdrecv.at[b]).wait_recv()
            item_out[b] += decode(crd.at[b], item_unit)
        return c

    lax.fori_loop(0, B, finish, 0)

    for j in range(1, Z):
        src = lax.rem(z + j, Z)
        vcopy(z, src, j - 1).wait_recv()
        user_out[pl.ds(pl.multiple_of(src * piece, piece), piece), :] = decode(ugr.at[src], user_unit)

    for d in range(1, Z):
        for way in (0, 1):
            pl.when(can_send(d, way))(lambda d=d, way=way: zcopy(d, way).wait_send())

    def drain(j, c):
        to = lax.rem(me + j, U)
        for p in range(Z):
            icopy(p, to, me).wait_send()
            gcopy(p, to, me).wait_send()
        return c

    lax.fori_loop(1, U, drain, 0)
    for j in range(1, Z):
        to = lax.rem(z + j, Z)
        ucopy(to, z).wait_send()
        vcopy(to, z, j - 1).wait_send()

        def drained(b, c):
            far("item", z, cs.at[to, b], cr.at[to, b], csend.at[to, b], crecv.at[to, b]).wait_send()
            return c
        lax.fori_loop(0, B, drained, 0)


def exchange(pick, items, user, feedback, U, Z):
    B, T, K = items.shape
    N = user.shape[0]
    piece = N // Z
    coded = T + PAD
    dma = pltpu.SemaphoreType.DMA
    i16 = jnp.int16
    vmem = pl.BlockSpec(memory_space=pltpu.VMEM)
    return pl.pallas_call(
        functools.partial(kernel, U, Z),
        out_shape=(jax.ShapeDtypeStruct((B, T, K), jnp.float32), jax.ShapeDtypeStruct((N, K), jnp.float32)),
        in_specs=[pl.BlockSpec(memory_space=pltpu.SMEM), vmem, vmem, pl.BlockSpec(memory_space=pl.ANY)],
        out_specs=(vmem, vmem),
        scratch_shapes=[pltpu.VMEM((B, T, K), jnp.bfloat16)] * (2 * (Z - 1)) + [
            pltpu.VMEM((Z, U, T, K), jnp.bfloat16),
            pltpu.VMEM((Z, U, T, K), jnp.bfloat16),
            pltpu.VMEM((Z, U, coded, K), i16),
            pltpu.VMEM((Z, U, coded, K), i16),
            pltpu.VMEM((Z, B, coded, K), i16),
            pltpu.VMEM((Z, B, coded, K), i16),
            pltpu.VMEM((B, coded, K), i16),
            pltpu.VMEM((2, 2, N, T), jnp.bfloat16),
            pltpu.VMEM((Z, piece + PAD, K), i16),
            pltpu.VMEM((Z, piece + PAD, K), i16),
            pltpu.VMEM((piece + PAD, K), i16),
            pltpu.VMEM((Z, piece + PAD, K), i16),
            pltpu.VMEM((N, K), jnp.float32),
            dma((2 * (Z - 1),)), dma((2 * (Z - 1),)),
            dma((Z, U)), dma((Z, U)), dma((Z, U)), dma((Z, U)),
            dma((Z, B)), dma((Z, B)), dma((B,)),
            dma((2,)),
            dma((Z,)), dma((Z,)), dma((Z,)), dma((Z,)),
        ],
        compiler_params=pltpu.CompilerParams(
            collective_id=0, has_side_effects=True, vmem_limit_bytes=63 * 2**20),
    )(pick, items, user, feedback)


def local(user_factors, item_factors, feedback, item_pick, user_noise, item_noise):
    U, Z = lax.axis_size("user"), lax.axis_size("item")
    tile, rank = feedback.shape[2], item_factors.shape[1]
    held = item_factors.shape[0] // tile
    items = item_factors.astype(jnp.bfloat16).reshape(held, tile, rank)
    item_grad, user_grad = exchange(
        item_pick, items, user_factors.astype(jnp.bfloat16),
        feedback.reshape(U, Z, feedback.shape[1], tile), U, Z)
    item_grad = item_grad.reshape(item_factors.shape)
    new_item = item_factors - item_step * (item_grad + prior_weight * item_factors) + item_noise_scale * item_noise
    new_user = user_factors - step_size * (user_grad + prior_weight * user_factors) + noise_scale * user_noise
    return (new_user, new_item)


def solution(mesh):
    in_specs = (
        P("user", None),
        P(("user", "item"), None),
        P("item", "user", None),
        P(),
        P("user", None),
        P(("user", "item"), None),
    )
    out_specs = (P("user", None), P(("user", "item"), None))
    return jax.shard_map(local, mesh=mesh, in_specs=in_specs, out_specs=out_specs, check_vma=False)
```

time: 158 us -> 140 us (0.89)
  Pallas kernels: 0 us -> 130 us
  waiting for transfers between devices: 97.1 us -> 0 us
  between operations: 14.1 us -> 0.65 us
  matrix products: 13.4 us -> 0 us
  starting transfers between devices: 11.9 us -> 0 us
  local copies, waits for them, and re-layouts: 10.9 us -> 0.01 us
    pallas_call x0 -> x1, Pallas kernels: none -> 130 us  [exchange(): pl.pallas_call(functools.partial(kernel, U, Z), out_shape=(jax.ShapeDtype...]
    psum x1 -> x0, waiting for transfers between devices: 54.9 us -> none  [local(): grad_total = lax.psum(user_grad, 'item')]
    all_to_all x2 -> x0, waiting for transfers between devices: 42.2 us -> none  [the longest x1 40.4 us: local(): lax.all_to_all(outgoing, ('user', 'item'), split_axis=0, concat_axis=0, t...]
    dot_general x4 -> x0, matrix products: 13.4 us -> none  [the longest x1 4.98 us: local(): jnp.einsum('nut,ntk->uk', residual, arrived, preferred_element_type=jnp.f...]
    all_to_all x2 -> x0, starting transfers between devices: 11.9 us -> none  [the longest x1 7.33 us: local(): lax.all_to_all(outgoing, ('user', 'item'), split_axis=0, concat_axis=0, t...]
    unnamed x12 -> x2, local copies, waits for them, and re-layouts: 10 us -> 0.01 us
    convert_element_type x1 -> x2, other arithmetic: 1.28 us -> 3.9 us  [the longest x1 2.07 us: local(): items = item_factors.astype(jnp.bfloat16).reshape(held, tile, rank)]
  transfers between devices with their start and end apart: 3 -> 0, of which waited for: 3 -> 0; matrix products, arithmetic and copies ran while one was open for 9% -> 0% of each run, Pallas kernels for 0% -> 0%
where the time goes in v2:
time: 140 us
  Pallas kernels  130 us (93%)
  other arithmetic  9.03 us (6%)
    pallas_call x1, Pallas kernels, exchange(): pl.pallas_call(functools.partial(kernel, U, Z), out_shape=(jax.ShapeDtype...  130 us
    add x1, other arithmetic, local(): item_factors - item_step * (item_grad + prior_weight * item_factors)  3.03 us

profile of v2, /device:TPU:0, one launch (start us, length us, event | category | flops | bytes accessed | tf_op | source)
XLA Modules:
  0.0 139.8 jit_solution(3635598906654494101)
XLA Ops:
  0.6 0.0 copy-start
  0.6 1.8 %convert_element_type.7.user = bf16[512,256]{1,0:T(8,128)(2,1)} convert(f32[512,256]{1,0:T(8,128)} %param.6) | non-fusion elementwise | flops 131072 | bytes 786432 | tf_op jit(solution)/shard_map/convert_element_type | solution.py:332
  2.5 2.1 %convert_element_type.6 = bf16[1024,256]{1,0:T(8,128)(2,1)} convert(f32[1024,256]{1,0:T(8,128)} %param.7) | non-fusion elementwise | flops 262144 | bytes 1572864 | tf_op jit(solution)/shard_map/convert_element_type | solution.py:330
  4.5 130.1 %shard_map.77 = (f32[8,128,256]{2,1,0:T(8,128)}, f32[512,256]{1,0:T(8,128)}) custom-call(s32[32,32]{1,0:T(8,128)} %pick.1, bf16[8,128,256]{2,1,0:T(8,128)(2,1)} %bitcast.11, bf16[512,256]{1,0:T(8,128)(2,1)} %convert_element_type.7.user, bf16[8,4,512,128]{3,2,1,0:T(8,128)(2,1)} %bitcast.10), custom_call_target="tpu_custom_call" | custom-call | tf_op jit(solution)/shard_map/pallas_call | solution.py:296
  134.6 0.0 copy-done
  134.7 2.1 %multiply_add_fusion = f32[512,256]{1,0:T(8,128)} fusion(f32[512,256]{1,0:T(8,128)} %param.10, f32[512,256]{1,0:T(8,128)S(1)} %copy-done, f32[512,256]{1,0:T(8,128)} %get-tuple-element.4), kind=kLoop, calls=%fused_computation.4 | loop fusion | flops 655360 | bytes 2097152 | tf_op jit(solution)/shard_map/add | solution.py:336
  136.8 3.0 %fusion.2 = f32[1024,256]{1,0:T(8,128)} fusion(f32[1024,256]{1,0:T(8,128)} %param.7, f32[8,128,256]{2,1,0:T(8,128)} %get-tuple-element.5, f32[1024,256]{1,0:T(8,128)} %param.11), kind=kLoop, calls=%fused_computation.3 | loop fusion | flops 1310720 | bytes 4194304 | tf_op jit(solution)/shard_map/add | solution.py:335
Async XLA Ops:
  0.6 134.0 %copy-start = (f32[512,256]{1,0:T(8,128)S(1)}, f32[512,256]{1,0:T(8,128)}, u32[]{:S(2)}) copy-start(f32[512,256]{1,0:T(8,128)} %param.6) | copy-start | bytes 1572868

commit v3 on v2

--- a/solution.py
+++ b/solution.py
@@ -152,26 +152,29 @@
             return c
         lax.fori_loop(1, U, one, 0)
 
-    def chain(p, way, relay):
+    def pass_on(p, b, way, relay):
+        to = z + (1 if way == 0 else -1)
+        total = dense(p, b)
+        if relay:
+            far("item", z, cs.at[p, b], cr.at[p, b], csend.at[p, b], crecv.at[p, b]).wait_recv()
+            total = total + decode(cr.at[p, b], item_unit)
+        encode(cs.at[p, b], total, item_unit)
+        if way == 0:
+            far("item", to, cs.at[p, b], cr.at[p, b], csend.at[p, b], crecv.at[p, b]).start()
+        else:
+            @pl.when(to == p)
+            def _():
+                far("item", to, cs.at[p, b], crd.at[b], csend.at[p, b], cdrecv.at[b]).start()
+
+            @pl.when(to != p)
+            def _():
+                far("item", to, cs.at[p, b], cr.at[p, b], csend.at[p, b], crecv.at[p, b]).start()
+
+    def chain(p, way):
         await_grads(p)
-        to = z + (1 if way == 0 else -1)
 
         def one(b, c):
-            total = dense(p, b)
-            if relay:
-                far("item", z, cs.at[p, b], cr.at[p, b], csend.at[p, b], crecv.at[p, b]).wait_recv()
-                total = total + decode(cr.at[p, b], item_unit)
-            encode(cs.at[p, b], total, item_unit)
-            if way == 0:
-                far("item", to, cs.at[p, b], cr.at[p, b], csend.at[p, b], crecv.at[p, b]).start()
-            else:
-                @pl.when(to == p)
-                def _():
-                    far("item", to, cs.at[p, b], crd.at[b], csend.at[p, b], cdrecv.at[b]).start()
-
-                @pl.when(to != p)
-                def _():
-                    far("item", to, cs.at[p, b], cr.at[p, b], csend.at[p, b], crecv.at[p, b]).start()
+            pass_on(p, b, way, False)
             return c
         lax.fori_loop(0, B, one, 0)
 
@@ -184,13 +187,10 @@
 
         @pl.when(comes(d, way) & edge)
         def _():
-            chain(plane(d, way), out, False)
-
-    steps = [(d, way) for d in range(1, Z) for way in (0, 1)]
+            chain(plane(d, way), out)
+
     spread(z, items)
-    last = None
-    older = None
-    compute_own = True
+    compute(z)
     for d in range(1, Z):
         for way in (0, 1):
             @pl.when(comes(d, way))
@@ -199,16 +199,11 @@
                 if d + 1 < Z:
                     pl.when(can_send(d + 1, way))(lambda: zcopy(d + 1, way).start())
                 spread(plane(d, way), zbufs[2 * (d - 1) + way])
-        if d == 1:
-            compute(z)
-        else:
+        if d > 1:
             for way in (0, 1):
-                pl.when(comes(d - 1, way))(lambda d=d, way=way: compute(plane(d - 1, way)))
-        if d > 2:
-            for way in (0, 1):
-                start_chain(d - 2, way)
-    for way in (0, 1):
-        pl.when(comes(Z - 1, way))(lambda way=way: compute(plane(Z - 1, way)))
+                start_chain(d - 1, way)
+        for way in (0, 1):
+            pl.when(comes(d, way))(lambda d=d, way=way: compute(plane(d, way)))
 
     def ucopy(to, src):
         return far("item", to, us.at[to], ur.at[src], usend.at[to], urecv.at[src])
@@ -217,27 +212,44 @@
         to = lax.rem(z + j, Z)
         encode(us.at[to], ug[pl.ds(pl.multiple_of(to * piece, piece), piece), :], user_unit)
         ucopy(to, z).start()
-    for d in range(max(Z - 2, 1), Z):
-        for way in (0, 1):
-            start_chain(d, way)
+    for way in (0, 1):
+        start_chain(Z - 1, way)
 
     def vcopy(to, src, j):
         return far("item", to, ugs, ugr.at[src], vsend.at[j], vrecv.at[src])
 
-    total = ug[pl.ds(pl.multiple_of(z * piece, piece), piece), :]
-    for j in range(1, Z):
-        src = lax.rem(z + j, Z)
-        ucopy(z, src).wait_recv()
-        total = total + decode(ur.at[src], user_unit)
-    encode(ugs, total, user_unit)
-    for j in range(1, Z):
-        vcopy(lax.rem(z + j, Z), z, j - 1).start()
-    user_out[pl.ds(pl.multiple_of(z * piece, piece), piece), :] = decode(ugs, user_unit)
-
-    for d in range(1, Z):
-        pl.when((z > 0) & (z + d < Z))(lambda d=d: chain(z + d, 0, True))
-    for d in range(1, Z):
-        pl.when((z < Z - 1) & (z - d >= 0))(lambda d=d: chain(z - d, 1, True))
+    def share_users():
+        total = ug[pl.ds(pl.multiple_of(z * piece, piece), piece), :]
+        for j in range(1, Z):
+            src = lax.rem(z + j, Z)
+            ucopy(z, src).wait_recv()
+            total = total + decode(ur.at[src], user_unit)
+        encode(ugs, total, user_unit)
+        for j in range(1, Z):
+            vcopy(lax.rem(z + j, Z), z, j - 1).start()
+        user_out[pl.ds(pl.multiple_of(z * piece, piece), piece), :] = decode(ugs, user_unit)
+
+    inner = (z > 0) & (z < Z - 1)
+    pl.when(inner)(lambda: [await_grads(lax.rem(z + j, Z)) for j in range(1, Z)] and None)
+
+    def relay(r):
+        def up(b):
+            pl.when(z < r)(lambda: pass_on(r, b, 0, True))
+
+        def down(b):
+            pl.when(z > Z - 1 - r)(lambda: pass_on(Z - 1 - r, b, 1, True))
+
+        def one(b, c):
+            pl.when(2 * z < Z - 1)(lambda: up(b))
+            down(b)
+            pl.when(2 * z >= Z - 1)(lambda: up(b))
+            return c
+        lax.fori_loop(0, B, one, 0)
+
+    for r in range(1, Z - 1):
+        pl.when(inner)(lambda r=r: relay(r))
+    share_users()
+    pl.when(inner)(lambda: relay(Z - 1))
 
     await_grads(z)
 

time: 140 us -> 129 us (0.921)
  Pallas kernels: 130 us -> 119 us
    pallas_call x1, Pallas kernels: 130 us -> 119 us  [exchange(): pl.pallas_call(functools.partial(kernel, U, Z), out_shape=(jax.ShapeDtype...]
where the time goes in v3:
time: 129 us
  Pallas kernels  119 us (92%)
  other arithmetic  9.03 us (7%)
    pallas_call x1, Pallas kernels, exchange(): pl.pallas_call(functools.partial(kernel, U, Z), out_shape=(jax.ShapeDtype...  119 us
    add x1, other arithmetic, local(): item_factors - item_step * (item_grad + prior_weight * item_factors)  3.03 us

profile of v3, /device:TPU:0, one launch (start us, length us, event | category | flops | bytes accessed | tf_op | source)
XLA Modules:
  0.0 128.7 jit_solution(11063033190161127320)
XLA Ops:
  0.6 0.0 copy-start
  0.6 1.8 %convert_element_type.7.user = bf16[512,256]{1,0:T(8,128)(2,1)} convert(f32[512,256]{1,0:T(8,128)} %param.6) | non-fusion elementwise | flops 131072 | bytes 786432 | tf_op jit(solution)/shard_map/convert_element_type | solution.py:344
  2.5 2.1 %convert_element_type.6 = bf16[1024,256]{1,0:T(8,128)(2,1)} convert(f32[1024,256]{1,0:T(8,128)} %param.7) | non-fusion elementwise | flops 262144 | bytes 1572864 | tf_op jit(solution)/shard_map/convert_element_type | solution.py:342
  4.5 119.0 %shard_map.77 = (f32[8,128,256]{2,1,0:T(8,128)}, f32[512,256]{1,0:T(8,128)}) custom-call(s32[32,32]{1,0:T(8,128)} %pick.1, bf16[8,128,256]{2,1,0:T(8,128)(2,1)} %bitcast.11, bf16[512,256]{1,0:T(8,128)(2,1)} %convert_element_type.7.user, bf16[8,4,512,128]{3,2,1,0:T(8,128)(2,1)} %bitcast.10), custom_call_target="tpu_custom_call" | custom-call | tf_op jit(solution)/shard_map/pallas_call | solution.py:308
  123.6 0.0 copy-done
  123.6 2.1 %multiply_add_fusion = f32[512,256]{1,0:T(8,128)} fusion(f32[512,256]{1,0:T(8,128)} %param.10, f32[512,256]{1,0:T(8,128)S(1)} %copy-done, f32[512,256]{1,0:T(8,128)} %get-tuple-element.4), kind=kLoop, calls=%fused_computation.4 | loop fusion | flops 655360 | bytes 2097152 | tf_op jit(solution)/shard_map/add | solution.py:348
  125.7 3.0 %fusion.2 = f32[1024,256]{1,0:T(8,128)} fusion(f32[1024,256]{1,0:T(8,128)} %param.7, f32[8,128,256]{2,1,0:T(8,128)} %get-tuple-element.5, f32[1024,256]{1,0:T(8,128)} %param.11), kind=kLoop, calls=%fused_computation.3 | loop fusion | flops 1310720 | bytes 4194304 | tf_op jit(solution)/shard_map/add | solution.py:347
Async XLA Ops:
  0.6 122.9 %copy-start = (f32[512,256]{1,0:T(8,128)S(1)}, f32[512,256]{1,0:T(8,128)}, u32[]{:S(2)}) copy-start(f32[512,256]{1,0:T(8,128)} %param.6) | copy-start | bytes 1572868

commit v4 on v3

--- a/solution.py
+++ b/solution.py
@@ -16,7 +16,7 @@
 
 FACTOR_BOUND = 1.5
 LEVELS = 32766.0
-PAD = 16
+PAD = 8
 
 
 def encode(ref, value, unit):
@@ -35,10 +35,10 @@
 
 
 def kernel(
-    U, Z, pick, items, user, feedback, item_out, user_out, *scratch
+    U, Z, pick, items_wide, user_wide, feedback, item_out, user_out, *scratch
 ):
     zbufs = scratch[: 2 * (Z - 1)]
-    (og, arr, gs, gr, cs, cr, crd, fb, us, ur, ugs, ugr, ug, zsend, zrecv, isend, irecv, gsend, grecv,
+    (items, user, og, arr, gs, gr, cs, cr, crd, fb, us, ur, ugs, ugr, ug, zsend, zrecv, isend, irecv, gsend, grecv,
      csend, crecv, cdrecv, fsem, usend, urecv, vsend, vrecv) = scratch[2 * (Z - 1):]
     B, T, K = items.shape
     N = user.shape[0]
@@ -55,6 +55,8 @@
 
     barrier = pltpu.get_barrier_semaphore()
 
+    items[...] = items_wide[...].astype(jnp.bfloat16)
+
     def greet_user(j, c):
         pl.semaphore_signal(barrier, inc=1, device_id={"user": lax.rem(me + j, U)}, device_id_type=pl.DeviceIdType.MESH)
         return c
@@ -78,6 +80,7 @@
     for way in (0, 1):
         pl.when(can_send(1, way))(lambda way=way: zcopy(1, way).start())
 
+    user[...] = user_wide[...].astype(jnp.bfloat16)
     ug[...] = jnp.zeros_like(ug)
 
     def icopy(p, to, src):
@@ -101,7 +104,7 @@
     pairs = U // 2
 
     def pair_of(j):
-        return lax.rem(me // 2 + 1 + j, pairs)
+        return lax.rem(me // 2 + pairs - j, pairs)
 
     def compute(p):
         fcopy(p, pair_of(0), 0).start()
@@ -199,11 +202,11 @@
                 if d + 1 < Z:
                     pl.when(can_send(d + 1, way))(lambda: zcopy(d + 1, way).start())
                 spread(plane(d, way), zbufs[2 * (d - 1) + way])
-        if d > 1:
-            for way in (0, 1):
-                start_chain(d - 1, way)
         for way in (0, 1):
             pl.when(comes(d, way))(lambda d=d, way=way: compute(plane(d, way)))
+        if d + 1 < Z:
+            for way in (0, 1):
+                start_chain(d, way)
 
     def ucopy(to, src):
         return far("item", to, us.at[to], ur.at[src], usend.at[to], urecv.at[src])
@@ -248,8 +251,8 @@
 
     for r in range(1, Z - 1):
         pl.when(inner)(lambda r=r: relay(r))
+    pl.when(inner)(lambda: relay(Z - 1))
     share_users()
-    pl.when(inner)(lambda: relay(Z - 1))
 
     await_grads(z)
 
@@ -310,7 +313,8 @@
         out_shape=(jax.ShapeDtypeStruct((B, T, K), jnp.float32), jax.ShapeDtypeStruct((N, K), jnp.float32)),
         in_specs=[pl.BlockSpec(memory_space=pltpu.SMEM), vmem, vmem, pl.BlockSpec(memory_space=pl.ANY)],
         out_specs=(vmem, vmem),
-        scratch_shapes=[pltpu.VMEM((B, T, K), jnp.bfloat16)] * (2 * (Z - 1)) + [
+        scratch_shapes=[pltpu.VMEM((B, T, K), jnp.bfloat16)] * (2 * (Z - 1) + 1) + [
+            pltpu.VMEM((N, K), jnp.bfloat16),
             pltpu.VMEM((Z, U, T, K), jnp.bfloat16),
             pltpu.VMEM((Z, U, T, K), jnp.bfloat16),
             pltpu.VMEM((Z, U, coded, K), i16),
@@ -339,9 +343,9 @@
     U, Z = lax.axis_size("user"), lax.axis_size("item")
     tile, rank = feedback.shape[2], item_factors.shape[1]
     held = item_factors.shape[0] // tile
-    items = item_factors.astype(jnp.bfloat16).reshape(held, tile, rank)
+    items = item_factors.reshape(held, tile, rank)
     item_grad, user_grad = exchange(
-        item_pick, items, user_factors.astype(jnp.bfloat16),
+        item_pick, items, user_factors,
         feedback.reshape(U, Z, feedback.shape[1], tile), U, Z)
     item_grad = item_grad.reshape(item_factors.shape)
     new_item = item_factors - item_step * (item_grad + prior_weight * item_factors) + item_noise_scale * item_noise

time: 129 us -> 122 us (0.946)
  other arithmetic: 9.03 us -> 5.13 us
  Pallas kernels: 119 us -> 116 us
    convert_element_type x2 -> x0, other arithmetic: 3.9 us -> none  [the longest x1 2.07 us: local(): items = item_factors.astype(jnp.bfloat16).reshape(held, tile, rank)]
    pallas_call x1, Pallas kernels: 119 us -> 116 us  [exchange(): pl.pallas_call(functools.partial(kernel, U, Z), out_shape=(jax.ShapeDtype...]
where the time goes in v4:
time: 122 us
  Pallas kernels  116 us (95%)
  other arithmetic  5.13 us (4%)
    pallas_call x1, Pallas kernels, exchange(): pl.pallas_call(functools.partial(kernel, U, Z), out_shape=(jax.ShapeDtype...  116 us
    add x1, other arithmetic, local(): item_factors - item_step * (item_grad + prior_weight * item_factors)  3.03 us

profile of v4, /device:TPU:0, one launch (start us, length us, event | category | flops | bytes accessed | tf_op | source)
XLA Modules:
  0.0 121.7 jit_solution(12445345820119859680)
XLA Ops:
  0.6 0.0 copy-start
  0.6 115.9 %shard_map.77 = (f32[8,128,256]{2,1,0:T(8,128)}, f32[512,256]{1,0:T(8,128)}) custom-call(s32[32,32]{1,0:T(8,128)} %pick.1, f32[8,128,256]{2,1,0:T(8,128)} %bitcast.11, f32[512,256]{1,0:T(8,128)} %user_wide.1, bf16[8,4,512,128]{3,2,1,0:T(8,128)(2,1)} %bitcast.10), custom_call_target="tpu_custom_call" | custom-call | tf_op jit(solution)/shard_map/pallas_call | solution.py:311
  116.6 0.0 copy-done
  116.6 2.1 %multiply_add_fusion = f32[512,256]{1,0:T(8,128)} fusion(f32[512,256]{1,0:T(8,128)} %param.10, f32[512,256]{1,0:T(8,128)S(1)} %copy-done, f32[512,256]{1,0:T(8,128)} %get-tuple-element.4), kind=kLoop, calls=%fused_computation.4 | loop fusion | flops 655360 | bytes 2097152 | tf_op jit(solution)/shard_map/add | solution.py:352
  118.7 3.0 %fusion.2 = f32[1024,256]{1,0:T(8,128)} fusion(f32[1024,256]{1,0:T(8,128)} %param.7, f32[8,128,256]{2,1,0:T(8,128)} %get-tuple-element.5, f32[1024,256]{1,0:T(8,128)} %param.11), kind=kLoop, calls=%fused_computation.3 | loop fusion | flops 1310720 | bytes 4194304 | tf_op jit(solution)/shard_map/add | solution.py:351
Async XLA Ops:
  0.6 116.0 %copy-start = (f32[512,256]{1,0:T(8,128)S(1)}, f32[512,256]{1,0:T(8,128)}, u32[]{:S(2)}) copy-start(f32[512,256]{1,0:T(8,128)} %user_wide.1) | copy-start | bytes 1572868

commit v5 on v4

--- a/solution.py
+++ b/solution.py
@@ -16,6 +16,7 @@
 
 FACTOR_BOUND = 1.5
 LEVELS = 32766.0
+RUN = 2
 PAD = 8
 
 
@@ -155,31 +156,41 @@
             return c
         lax.fori_loop(1, U, one, 0)
 
-    def pass_on(p, b, way, relay):
+    def run(b):
+        return pl.ds(b * RUN, RUN)
+
+    def up_copy(to, p, c):
+        return far("item", to, cs.at[p, run(c)], cr.at[p, run(c)], csend.at[p, c], crecv.at[p, c])
+
+    def last_copy(to, p, c):
+        return far("item", to, cs.at[p, run(c)], crd.at[run(c)], csend.at[p, c], cdrecv.at[c])
+
+    def pass_on(p, c, way, relay):
         to = z + (1 if way == 0 else -1)
-        total = dense(p, b)
         if relay:
-            far("item", z, cs.at[p, b], cr.at[p, b], csend.at[p, b], crecv.at[p, b]).wait_recv()
-            total = total + decode(cr.at[p, b], item_unit)
-        encode(cs.at[p, b], total, item_unit)
+            up_copy(z, p, c).wait_recv()
+
+        def one(i, carry):
+            b = c * RUN + i
+            total = dense(p, b)
+            if relay:
+                total = total + decode(cr.at[p, b], item_unit)
+            encode(cs.at[p, b], total, item_unit)
+            return carry
+        lax.fori_loop(0, RUN, one, 0)
         if way == 0:
-            far("item", to, cs.at[p, b], cr.at[p, b], csend.at[p, b], crecv.at[p, b]).start()
+            up_copy(to, p, c).start()
         else:
-            @pl.when(to == p)
-            def _():
-                far("item", to, cs.at[p, b], crd.at[b], csend.at[p, b], cdrecv.at[b]).start()
-
-            @pl.when(to != p)
-            def _():
-                far("item", to, cs.at[p, b], cr.at[p, b], csend.at[p, b], crecv.at[p, b]).start()
+            pl.when(to == p)(lambda: last_copy(to, p, c).start())
+            pl.when(to != p)(lambda: up_copy(to, p, c).start())
 
     def chain(p, way):
         await_grads(p)
 
-        def one(b, c):
-            pass_on(p, b, way, False)
-            return c
-        lax.fori_loop(0, B, one, 0)
+        def one(c, carry):
+            pass_on(p, c, way, False)
+            return carry
+        lax.fori_loop(0, B // RUN, one, 0)
 
     def plane(d, way):
         return z - d if way == 0 else z + d
@@ -247,7 +258,7 @@
             down(b)
             pl.when(2 * z >= Z - 1)(lambda: up(b))
             return c
-        lax.fori_loop(0, B, one, 0)
+        lax.fori_loop(0, B // RUN, one, 0)
 
     for r in range(1, Z - 1):
         pl.when(inner)(lambda r=r: relay(r))
@@ -261,12 +272,12 @@
 
         @pl.when(z > 0)
         def _():
-            far("item", z, cs.at[z, b], cr.at[z, b], csend.at[z, b], crecv.at[z, b]).wait_recv()
+            pl.when(lax.rem(b, RUN) == 0)(lambda: up_copy(z, z, b // RUN).wait_recv())
             item_out[b] += decode(cr.at[z, b], item_unit)
 
         @pl.when(z < Z - 1)
         def _():
-            far("item", z, cs.at[z, b], crd.at[b], csend.at[z, b], cdrecv.at[b]).wait_recv()
+            pl.when(lax.rem(b, RUN) == 0)(lambda: last_copy(z, z, b // RUN).wait_recv())
             item_out[b] += decode(crd.at[b], item_unit)
         return c
 
@@ -295,9 +306,9 @@
         vcopy(to, z, j - 1).wait_send()
 
         def drained(b, c):
-            far("item", z, cs.at[to, b], cr.at[to, b], csend.at[to, b], crecv.at[to, b]).wait_send()
-            return c
-        lax.fori_loop(0, B, drained, 0)
+            up_copy(z, to, b).wait_send()
+            return c
+        lax.fori_loop(0, B // RUN, drained, 0)
 
 
 def exchange(pick, items, user, feedback, U, Z):
@@ -330,7 +341,7 @@
             pltpu.VMEM((N, K), jnp.float32),
             dma((2 * (Z - 1),)), dma((2 * (Z - 1),)),
             dma((Z, U)), dma((Z, U)), dma((Z, U)), dma((Z, U)),
-            dma((Z, B)), dma((Z, B)), dma((B,)),
+            dma((Z, B // RUN)), dma((Z, B // RUN)), dma((B // RUN,)),
             dma((2,)),
             dma((Z,)), dma((Z,)), dma((Z,)), dma((Z,)),
         ],

time: 122 us -> 116 us (0.951)
  Pallas kernels: 116 us -> 110 us
    pallas_call x1, Pallas kernels: 116 us -> 110 us  [exchange(): pl.pallas_call(functools.partial(kernel, U, Z), out_shape=(jax.ShapeDtype...]
where the time goes in v5:
time: 116 us
  Pallas kernels  110 us (95%)
  other arithmetic  5.13 us (4%)
    pallas_call x1, Pallas kernels, exchange(): pl.pallas_call(functools.partial(kernel, U, Z), out_shape=(jax.ShapeDtype...  110 us
    add x1, other arithmetic, local(): item_factors - item_step * (item_grad + prior_weight * item_factors)  3.03 us

profile of v5, /device:TPU:0, one launch (start us, length us, event | category | flops | bytes accessed | tf_op | source)
XLA Modules:
  0.0 116.1 jit_solution(8673348716109480151)
XLA Ops:
  0.6 0.0 copy-start
  0.6 110.3 %shard_map.77 = (f32[8,128,256]{2,1,0:T(8,128)}, f32[512,256]{1,0:T(8,128)}) custom-call(s32[32,32]{1,0:T(8,128)} %pick.1, f32[8,128,256]{2,1,0:T(8,128)} %bitcast.11, f32[512,256]{1,0:T(8,128)} %user_wide.1, bf16[8,4,512,128]{3,2,1,0:T(8,128)(2,1)} %bitcast.10), custom_call_target="tpu_custom_call" | custom-call | tf_op jit(solution)/shard_map/pallas_call | solution.py:322
  111.0 0.0 copy-done
  111.0 2.1 %multiply_add_fusion = f32[512,256]{1,0:T(8,128)} fusion(f32[512,256]{1,0:T(8,128)} %param.10, f32[512,256]{1,0:T(8,128)S(1)} %copy-done, f32[512,256]{1,0:T(8,128)} %get-tuple-element.4), kind=kLoop, calls=%fused_computation.4 | loop fusion | flops 655360 | bytes 2097152 | tf_op jit(solution)/shard_map/add | solution.py:363
  113.1 3.0 %fusion.2 = f32[1024,256]{1,0:T(8,128)} fusion(f32[1024,256]{1,0:T(8,128)} %param.7, f32[8,128,256]{2,1,0:T(8,128)} %get-tuple-element.5, f32[1024,256]{1,0:T(8,128)} %param.11), kind=kLoop, calls=%fused_computation.3 | loop fusion | flops 1310720 | bytes 4194304 | tf_op jit(solution)/shard_map/add | solution.py:362
Async XLA Ops:
  0.6 110.3 %copy-start = (f32[512,256]{1,0:T(8,128)S(1)}, f32[512,256]{1,0:T(8,128)}, u32[]{:S(2)}) copy-start(f32[512,256]{1,0:T(8,128)} %user_wide.1) | copy-start | bytes 1572868
